TPU v7x, 256 devices: a whole 4x4x8 slice. The times are simulated.
256 devices in a mesh: sec: 32 (over z, y), depth: 4 (over x), segment: 2 (over core).
Axes of the slice: x: 4, y: 4, z: 8, core: 2. Of those that a mesh axis runs over, the one named last changes fastest.
Arguments:
- fields: float32 [2, 9, 64, 64, 128], P('segment', None, 'sec', 'depth'), may hold values from -6 to 6
- block_ids: int32 [2, 64, 64, 128], P('segment', 'sec', 'depth'), may hold values from 0 to 15
- buoyancy: float32 [16], replicated, may hold values from 0.5 to 1
- lame_lambda: float32 [16], replicated, may hold values from 0.2 to 0.6
- lame_mu: float32 [16], replicated, may hold values from 0.1 to 0.3
- moments: float32 [6, 131072], P(None, ('sec', 'depth')), may hold values from -12 to 12
- moment_owner: int32 [131072, 1], P(('sec', 'depth')), may hold values from 0 to 31; in each aligned block of 1024 rows (0 to 1023, 1024 to 2047, ...) at most 64 rows name the same one
- moment_cells: int32 [131072], P(('sec', 'depth')), may hold values from 0 to 4095
- drm_rows: int32 [262144], P(('sec', 'depth')), may hold values from 0 to 4095
Outputs:
- final_fields: float32 [2, 9, 64, 64, 128], P('segment', None, 'sec', 'depth')
Inputs may be any that keep to these rules, and one draw needn't show every extreme that they name: `moment_owner`: in the entries of one section and slab at most 64 name the same section, a bound that some block reaches of them.
All inputs are finite; a program needn't handle non-finite values.
Results may differ from a plain program's by a relative error of at most 0.00002.
Values sent between devices are 32-bit elements; how exact they have to be, the bound alone decides.
A program may use at most 64 MiB of HBM per device.

v0:
```python
import jax
import jax.numpy as jnp
from jax import lax
from jax.sharding import PartitionSpec as P

STEPS = 4
HALF_STEP = 0.5


def passed_along(block, axis, distance):
    devices = range(lax.axis_size(axis))
    route = [(i - distance, i) for i in devices if i - distance in devices]
    return lax.ppermute(block, axis, route)


def lookup(block_ids, table):
    result = jnp.zeros(block_ids.shape, jnp.float32)
    for entry in range(table.shape[0]):
        result = result + jnp.where(block_ids == entry, table[entry], jnp.float32(0.0))
    return result


def back_diff(field, before_rim, axis):
    count = field.shape[axis]
    before = jnp.concatenate([before_rim, lax.slice_in_dim(field, 0, count - 1, axis=axis)], axis)
    return field - before


def fore_diff(field, after_rim, axis):
    count = field.shape[axis]
    after = jnp.concatenate([lax.slice_in_dim(field, 1, count, axis=axis), after_rim], axis)
    return after - field


def stress_rims(state):
    xplane = jnp.stack([state[:, 3, -1:], state[:, 8, -1:], state[:, 7, -1:]], axis=1)
    zplane = jnp.stack([state[:, 7, :, -1:], state[:, 6, :, -1:], state[:, 5, :, -1:]], axis=1)
    x_rims = passed_along(xplane, "sec", 1)
    z_rims = passed_along(zplane, "depth", 1)
    return (x_rims, z_rims)


def velocity_rims(newv):
    xplane = newv[:, :, :1]
    zplane = newv[:, :, :, :1]
    x_rims = passed_along(xplane, "sec", -1)
    z_rims = passed_along(zplane, "depth", -1)
    return (x_rims, z_rims)


def couple(newv, oldv, rows_here):
    shape_one = newv.shape[1:]
    increment = (newv[0] - oldv[0]).reshape(3, -1)[:, rows_here]
    arrived = passed_along(increment, "segment", 1)
    basin = newv[0].reshape(3, -1).at[:, rows_here].add(arrived)
    return basin.reshape((1,) + shape_one)


def advance(state, buoy, lam, shear, rows_here):
    x_rims, z_rims = stress_rims(state)
    vx, vy, vz = (state[:, 0], state[:, 1], state[:, 2])
    sxx, syy, szz, syz, sxz, sxy = (state[:, k] for k in range(3, 9))
    y_zero = jnp.zeros_like(sxx[..., :1])
    nvx = vx + HALF_STEP * buoy * (
        back_diff(sxx, x_rims[:, 0], 1)
        + back_diff(sxy, y_zero, 3)
        + back_diff(sxz, z_rims[:, 0], 2)
    )
    nvy = vy + HALF_STEP * buoy * (
        back_diff(sxy, x_rims[:, 1], 1)
        + back_diff(syy, y_zero, 3)
        + back_diff(syz, z_rims[:, 1], 2)
    )
    nvz = vz + HALF_STEP * buoy * (
        back_diff(sxz, x_rims[:, 2], 1)
        + back_diff(syz, y_zero, 3)
        + back_diff(szz, z_rims[:, 2], 2)
    )
    newv = couple(jnp.stack([nvx, nvy, nvz], axis=1), state[:, :3], rows_here)
    vx_rims, vz_rims = velocity_rims(newv)
    vx, vy, vz = (newv[:, 0], newv[:, 1], newv[:, 2])
    exx = fore_diff(vx, vx_rims[:, 0], 1)
    eyy = fore_diff(vy, y_zero, 3)
    ezz = fore_diff(vz, vz_rims[:, 2], 2)
    trace = exx + eyy + ezz
    sxx = sxx + HALF_STEP * (lam * trace + 2.0 * shear * exx)
    syy = syy + HALF_STEP * (lam * trace + 2.0 * shear * eyy)
    szz = szz + HALF_STEP * (lam * trace + 2.0 * shear * ezz)
    syz = syz + HALF_STEP * shear * (fore_diff(vy, vz_rims[:, 1], 2) + fore_diff(vz, y_zero, 3))
    sxz = sxz + HALF_STEP * shear * (
        fore_diff(vx, vz_rims[:, 0], 2) + fore_diff(vz, vx_rims[:, 2], 1)
    )
    sxy = sxy + HALF_STEP * shear * (fore_diff(vx, y_zero, 3) + fore_diff(vy, vx_rims[:, 1], 1))
    return jnp.stack([vx, vy, vz, sxx, syy, szz, syz, sxz, sxy], axis=1)


def on_device(
    fields, block_ids, buoyancy, lame_lambda, lame_mu, moments, moment_owner, moment_cells, drm_rows
):
    my_section = lax.axis_index("sec")
    segment_pos = lax.axis_index("segment")
    width_x, width_z, width_y = (fields.shape[2], fields.shape[3], fields.shape[4])
    cells_here = width_x * width_z * width_y
    all_moments, all_owner, all_cells = (
        lax.all_gather(moments, "sec", axis=1, tiled=True),
        lax.all_gather(moment_owner, "sec", axis=0, tiled=True),
        lax.all_gather(moment_cells, "sec", axis=0, tiled=True),
    )
    values = all_moments
    places = jnp.where(all_owner[:, 0] == my_section, all_cells, cells_here)
    values = values * (segment_pos == 0).astype(jnp.float32)
    stress = fields[0, 3:].reshape(6, -1).at[:, places].add(values, mode="drop")
    state = jnp.concatenate(
        [fields[:, :3], stress.reshape(1, 6, width_x, width_z, width_y)], axis=1
    )
    block_here = block_ids[:, None]
    block_here = block_here[:, 0]
    buoy = lookup(block_here, buoyancy)
    lam = lookup(block_here, lame_lambda)
    shear = lookup(block_here, lame_mu)
    for step in range(STEPS):
        state = advance(state, buoy, lam, shear, drm_rows)
    return state


def solution(mesh):
    in_specs = (
        P("segment", None, "sec", "depth", None),
        P("segment", "sec", "depth", None),
        P(),
        P(),
        P(),
        P(None, ("sec", "depth")),
        P(("sec", "depth"), None),
        P(("sec", "depth")),
        P(("sec", "depth")),
    )
    out_specs = P("segment", None, "sec", "depth", None)
    return jax.shard_map(
        on_device, mesh=mesh, in_specs=in_specs, out_specs=out_specs, check_vma=False
    )
```

profile of v0, /device:TPU:124, one launch (start us, length us, event | category | flops | bytes accessed | tf_op | source)
XLA Modules:
  0.0 604.5 jit_solution(15526155525644759450)
XLA Ops:
  0.0 49.8 %all_gather.11 = f32[6,32768]{1,0:T(8,128)S(1)} all-gather(f32[6,1024]{1,0:T(8,128)} %param.14), channel_id=1, replica_groups=mesh['sec'=32,'depth'=4,'segment'=2] {'sec'}, dimensions={1}, use_global_device_ids=true | all-gather | bytes 811008 | tf_op jit(solution)/shard_map/all_gather | solution.py:105
  50.0 8.9 %copy.799 = f32[32768,6]{1,0:T(8,128)} copy(f32[32768,6]{0,1:T(8,128)S(1)} %multiply_bitcast_fusion) | data formatting | bytes 1572864 | tf_op jit(solution)/shard_map/mul | solution.py:111
  58.9 41.3 %all_gather.9 = s32[32768,1]{0,1:T(1,128)S(1)} all-gather(s32[1024,1]{0,1:T(1,128)S(1)} %copy-done.12), channel_id=1, replica_groups=mesh['sec'=32,'depth'=4,'segment'=2] {'sec'}, dimensions={0}, use_global_device_ids=true | all-gather | bytes 135168 | tf_op jit(solution)/shard_map/all_gather | solution.py:106
  100.1 42.0 %all_gather.10 = s32[32768]{0:T(1024)S(1)} all-gather(s32[1024]{0:T(1024)S(1)} %copy-done.13), channel_id=1, replica_groups=mesh['sec'=32,'depth'=4,'segment'=2] {'sec'}, dimensions={0}, use_global_device_ids=true | all-gather | bytes 135168 | tf_op jit(solution)/shard_map/all_gather | solution.py:107
  143.2 175.0 %scatter_fusion = f32[6,4096]{0,1:T(8,128)S(1)} fusion(f32[6,4096]{0,1:T(8,128)S(1)} %bitcast.376, s32[32768]{0:T(1024)S(1)} %compare_select_fusion, f32[32768,6]{1,0:T(8,128)} %copy.799), kind=kCustom, calls=%fused_computation.4 | custom fusion | flops 196608 | bytes 2490368 | tf_op jit(solution)/shard_map/scatter-add | solution.py:112
  327.3 4.7 collective-permute-start
  332.0 7.3 %fusion.93 = (f32[1,1,2,16,128]{1,4,3,2,0:T(8,128)}, f32[1,1,2,16,128]{1,4,3,2,0:T(8,128)}, f32[1,1,2,16,128]{1,4,3,2,0:T(8,128)}, f32[1,1,2,16,128]{1,4,3,2,0:T...) fusion(f32[1,6,2,16,128]{1,4,3,2,0:T(8,128)S(1)} %bitcast.379), kind=kLoop, calls=%fused_computation.240 | loop fusion | bytes 196608 | tf_op jit(solution)/shard_map/slice | solution.py:62
  353.3 10.7 %fusion.3 = (f32[1,2,16,128]{3,2,1,0:T(8,128)S(1)}, f32[1,2,16,128]{3,2,1,0:T(8,128)S(1)}, pred[1,2,16,128]{3,2,1,0:T(8,128)(4,1)S(1)}, pred[1,2,16,128]{3,2,1,0...) fusion(f32[1,1,16,128]{3,2,1,0:T(8,128)S(1)} %slice.912, ...), kind=kLoop, calls=%fused_computation.29 | loop fusion | flops 233472 | bytes 229312 | tf_op jit(solution)/shard_map/add | solution.py:64
  367.9 7.0 %gather_fusion = f32[2048,3]{1,0:T(8,128)S(1)} fusion(f32[3,4096]{0,1:T(8,128)} %bitcast_subtract_fusion, s32[2048]{0:T(1024)S(1)} %get-tuple-element.103), kind=kCustom, calls=%fused_computation | custom fusion | bytes 57344 | tf_op jit(solution)/shard_map/gather | solution.py:53
  377.9 12.2 %scatter_fusion.1 = f32[3,4096]{0,1:T(8,128)S(1)} fusion(f32[3,4096]{0,1:T(8,128)S(1)} %copy.807, s32[2048]{0:T(1024)S(1)} %get-tuple-element.104, f32[2048,3]{1,0:T(8,128)S(1)} %copy.808), kind=kCustom, calls=%fused_computation.5 | custom fusion | flops 6144 | bytes 81920 | tf_op jit(solution)/shard_map/scatter-add | solution.py:55
  393.0 4.0 fusion.92
  406.2 7.1 %collective-permute-done.3 = f32[1,3,1,16,128]{4,3,2,1,0:T(8,128)S(1)} collective-permute-done((f32[1,3,1,16,128]{4,3,2,1,0:T(8,128)S(1)}, f32[1,3,1,16,128]{4,3,2,1,0:T(8,128)S(1)}, u32[]{:S(2)}, u32[]{:S(2)}) %collective-permute-start.3) | collective-permute-done | bytes 24608 | tf_op jit(solution)/shard_map/ppermute | solution.py:13
  413.3 20.5 %multiply_add_fusion.6 = (f32[1,2,16,128]{3,2,1,0:T(8,128)S(1)}, f32[1,2,16,128]{3,2,1,0:T(8,128)S(1)}, f32[1,2,16,128]{3,2,1,0:T(8,128)S(1)}, f32[1,2,16,128]{3,2,1,0:T(8,128)S(1)}) fusion(f32[1,2,16,127]{3,2,1,0:T(8,128)S(1)} %slice.939, f32[1,1,2,16,128]{4,3,2,1,0:T(8,128)S(1)} %copy.875, f32[1,1,2,16,128]{4,3,2,1,0:T(8,128)S(1)} %copy.870, ...), kind=kLoop, calls=%fused_computation.178 | loop fusion | flops 307200 | bytes 245760 | tf_op jit(solution)/shard_map/add | solution.py:87
  448.2 7.2 %gather_fusion.1 = f32[2048,3]{1,0:T(8,128)S(1)} fusion(f32[3,4096]{0,1:T(8,128)} %sub.500, s32[2048]{0:T(1024)S(1)} %get-tuple-element.103), kind=kCustom, calls=%fused_computation.1 | custom fusion | bytes 57344 | tf_op jit(solution)/shard_map/gather | solution.py:53
  458.2 12.2 %scatter_fusion.2 = f32[3,4096]{0,1:T(8,128)S(1)} fusion(f32[3,4096]{0,1:T(8,128)S(1)} %copy-done, s32[2048]{0:T(1024)S(1)} %get-tuple-element.104, f32[2048,3]{1,0:T(8,128)S(1)} %copy.821), kind=kCustom, calls=%fused_computation.6 | custom fusion | flops 6144 | bytes 81920 | tf_op jit(solution)/shard_map/scatter-add | solution.py:55
  473.3 4.0 fusion.91
  486.6 7.1 %collective-permute-done.8 = f32[1,3,1,16,128]{4,3,2,1,0:T(8,128)S(1)} collective-permute-done((f32[1,3,1,16,128]{4,3,2,1,0:T(8,128)S(1)}, f32[1,3,1,16,128]{4,3,2,1,0:T(8,128)S(1)}, u32[]{:S(2)}, u32[]{:S(2)}) %collective-permute-start.8) | collective-permute-done | bytes 24608 | tf_op jit(solution)/shard_map/ppermute | solution.py:13
  508.1 7.2 %gather_fusion.2 = f32[2048,3]{1,0:T(8,128)S(1)} fusion(f32[3,4096]{0,1:T(8,128)} %sub.519, s32[2048]{0:T(1024)S(1)} %get-tuple-element.103), kind=kCustom, calls=%fused_computation.2 | custom fusion | bytes 57344 | tf_op jit(solution)/shard_map/gather | solution.py:53
  518.1 12.2 %scatter_fusion.3 = f32[3,4096]{0,1:T(8,128)S(1)} fusion(f32[3,4096]{0,1:T(8,128)S(1)} %copy-done.1, s32[2048]{0:T(1024)S(1)} %get-tuple-element.104, f32[2048,3]{1,0:T(8,128)S(1)} %copy.834), kind=kCustom, calls=%fused_computation.7 | custom fusion | flops 6144 | bytes 81920 | tf_op jit(solution)/shard_map/scatter-add | solution.py:55
  533.2 4.0 fusion.90
  546.5 7.1 %collective-permute-done.13 = f32[1,3,1,16,128]{4,3,2,1,0:T(8,128)S(1)} collective-permute-done((f32[1,3,1,16,128]{4,3,2,1,0:T(8,128)S(1)}, f32[1,3,1,16,128]{4,3,2,1,0:T(8,128)S(1)}, u32[]{:S(2)}, u32[]{:S(2)}) %collective-permute-start.13) | collective-permute-done | bytes 24608 | tf_op jit(solution)/shard_map/ppermute | solution.py:13
  568.0 7.2 %gather_fusion.3 = f32[2048,3]{1,0:T(8,128)S(1)} fusion(f32[3,4096]{0,1:T(8,128)} %sub.538, s32[2048]{0:T(1024)S(1)} %get-tuple-element.103), kind=kCustom, calls=%fused_computation.3 | custom fusion | bytes 57344 | tf_op jit(solution)/shard_map/gather | solution.py:53
  578.0 12.2 %scatter_fusion.4 = f32[3,4096]{0,1:T(8,128)S(1)} fusion(f32[3,4096]{0,1:T(8,128)S(1)} %copy-done.2, s32[2048]{0:T(1024)S(1)} %get-tuple-element.104, f32[2048,3]{1,0:T(8,128)S(1)} %copy.847), kind=kCustom, calls=%fused_computation.8 | custom fusion | flops 6144 | bytes 81920 | tf_op jit(solution)/shard_map/scatter-add | solution.py:55
  596.5 6.6 %collective-permute-done.18 = f32[1,3,1,16,128]{4,3,2,1,0:T(8,128)S(1)} collective-permute-done((f32[1,3,1,16,128]{4,3,2,1,0:T(8,128)S(1)}, f32[1,3,1,16,128]{4,3,2,1,0:T(8,128)S(1)}, u32[]{:S(2)}, u32[]{:S(2)}) %collective-permute-start.18) | collective-permute-done | bytes 24608 | tf_op jit(solution)/shard_map/ppermute | solution.py:13
  (246 shorter events, 125.9 us)
Async XLA Ops:
  49.9 50.2 %copy-start.13 = (s32[1024]{0:T(1024)S(1)}, s32[1024]{0:T(1024)}, u32[]{:S(2)}) copy-start(s32[1024]{0:T(1024)} %param.16) | copy-start | bytes 12292
  49.9 92.2 %slice-start = ((f32[1,9,2,16,128]{4,3,2,1,0:T(8,128)}), f32[1,6,2,16,128]{4,3,2,1,0:T(8,128)S(1)}, s32[]{:S(2)}) async-start(f32[1,9,2,16,128]{4,3,2,1,0:T(8,128)} %param.9), calls=%async_computation | async-start | bytes 196608 | tf_op jit(solution)/shard_map/slice | solution.py:112
  318.7 34.6 %collective-permute-start.1 = (f32[1,3,2,1,128]{4,3,2,1,0:T(1,128)S(1)}, f32[1,3,2,1,128]{4,3,2,1,0:T(1,128)S(1)}, u32[]{:S(2)}, u32[]{:S(2)}) collective-permute-start(f32[1,3,2,1,128]{4,3,2,1,0:T(1,128)S(1)} %pad_maximum_fusion.8), channel_id=1, source_target_pairs={{0,2},{2,4},{4,6},{1,3},{3,5},{5,7},{8,10},{10,12},{12,14},{9,11},... | collective-permute-start | bytes 9224 | tf_op jit(solution)/shard_map/ppermute | solution.py:13
  327.2 12.8 %copy-start.11 = (s32[2048]{0:T(1024)S(1)}, s32[2048]{0:T(1024)}, u32[]{:S(2)}) copy-start(s32[2048]{0:T(1024)} %param.17) | copy-start | bytes 24580
  327.3 12.8 %copy-start.7 = (f32[16]{0:T(128)S(1)}, f32[16]{0:T(128)}, u32[]{:S(2)}) copy-start(f32[16]{0:T(128)} %param.12) | copy-start | bytes 196
  327.3 26.0 %collective-permute-start = (f32[1,3,1,16,128]{4,3,2,1,0:T(8,128)S(1)}, f32[1,3,1,16,128]{4,3,2,1,0:T(8,128)S(1)}, u32[]{:S(2)}, u32[]{:S(2)}) collective-permute-start(f32[1,3,1,16,128]{4,3,2,1,0:T(8,128)S(1)} %pad_maximum_fusion.4), channel_id=1, source_target_pairs={{0,8},{8,16},{16,24},{24,32},{32,40},{40,48},{48,56},{56,64},{64,7... | collective-permute-start | bytes 73736 | tf_op jit(solution)/shard_map/ppermute | solution.py:13
  375.3 2.2 collective-permute-start.2
  390.2 16.0 %collective-permute-start.4 = (f32[1,3,2,1,128]{4,2,3,1,0:T(2,128)S(1)}, f32[1,3,2,1,128]{4,2,3,1,0:T(2,128)S(1)}, u32[]{:S(2)}, u32[]{:S(2)}) collective-permute-start(f32[1,3,2,1,128]{4,2,3,1,0:T(2,128)S(1)} %copy.877), channel_id=1, source_target_pairs={{2,0},{4,2},{6,4},{3,1},{5,3},{7,5},{10,8},{12,10},{14,12},{11,9},... | collective-permute-start | bytes 9224 | tf_op jit(solution)/shard_map/ppermute | solution.py:13
  404.3 9.0 %collective-permute-start.3 = (f32[1,3,1,16,128]{4,3,2,1,0:T(8,128)S(1)}, f32[1,3,1,16,128]{4,3,2,1,0:T(8,128)S(1)}, u32[]{:S(2)}, u32[]{:S(2)}) collective-permute-start(f32[1,3,1,16,128]{4,3,2,1,0:T(8,128)S(1)} %copy.874), channel_id=1, source_target_pairs={{8,0},{16,8},{24,16},{32,24},{40,32},{48,40},{56,48},{64,56},{72,6... | collective-permute-start | bytes 73736 | tf_op jit(solution)/shard_map/ppermute | solution.py:13
  433.9 5.5 collective-permute-start.6
  437.1 5.7 collective-permute-start.5
  455.7 2.1 collective-permute-start.7
  470.6 16.0 %collective-permute-start.9 = (f32[1,3,2,1,128]{4,2,3,1,0:T(2,128)S(1)}, f32[1,3,2,1,128]{4,2,3,1,0:T(2,128)S(1)}, u32[]{:S(2)}, u32[]{:S(2)}) collective-permute-start(f32[1,3,2,1,128]{4,2,3,1,0:T(2,128)S(1)} %copy.885), channel_id=1, source_target_pairs={{2,0},{4,2},{6,4},{3,1},{5,3},{7,5},{10,8},{12,10},{14,12},{11,9},... | collective-permute-start | bytes 9224 | tf_op jit(solution)/shard_map/ppermute | solution.py:13
  484.6 9.0 %collective-permute-start.8 = (f32[1,3,1,16,128]{4,3,2,1,0:T(8,128)S(1)}, f32[1,3,1,16,128]{4,3,2,1,0:T(8,128)S(1)}, u32[]{:S(2)}, u32[]{:S(2)}) collective-permute-start(f32[1,3,1,16,128]{4,3,2,1,0:T(8,128)S(1)} %copy.882), channel_id=1, source_target_pairs={{8,0},{16,8},{24,16},{32,24},{40,32},{48,40},{56,48},{64,56},{72,6... | collective-permute-start | bytes 73736 | tf_op jit(solution)/shard_map/ppermute | solution.py:13
  493.8 5.5 collective-permute-start.11
  497.0 5.7 collective-permute-start.10
  515.6 2.1 collective-permute-start.12
  530.5 16.0 %collective-permute-start.14 = (f32[1,3,2,1,128]{4,2,3,1,0:T(2,128)S(1)}, f32[1,3,2,1,128]{4,2,3,1,0:T(2,128)S(1)}, u32[]{:S(2)}, u32[]{:S(2)}) collective-permute-start(f32[1,3,2,1,128]{4,2,3,1,0:T(2,128)S(1)} %copy.893), channel_id=1, source_target_pairs={{2,0},{4,2},{6,4},{3,1},{5,3},{7,5},{10,8},{12,10},{14,12},{11,9},... | collective-permute-start | bytes 9224 | tf_op jit(solution)/shard_map/ppermute | solution.py:13
  544.5 9.0 %collective-permute-start.13 = (f32[1,3,1,16,128]{4,3,2,1,0:T(8,128)S(1)}, f32[1,3,1,16,128]{4,3,2,1,0:T(8,128)S(1)}, u32[]{:S(2)}, u32[]{:S(2)}) collective-permute-start(f32[1,3,1,16,128]{4,3,2,1,0:T(8,128)S(1)} %copy.890), channel_id=1, source_target_pairs={{8,0},{16,8},{24,16},{32,24},{40,32},{48,40},{56,48},{64,56},{72,6... | collective-permute-start | bytes 73736 | tf_op jit(solution)/shard_map/ppermute | solution.py:13
  553.7 5.5 collective-permute-start.16
  556.9 5.7 collective-permute-start.15
  575.5 2.1 collective-permute-start.17
  591.0 5.5 collective-permute-start.19
  594.0 9.0 %collective-permute-start.18 = (f32[1,3,1,16,128]{4,3,2,1,0:T(8,128)S(1)}, f32[1,3,1,16,128]{4,3,2,1,0:T(8,128)S(1)}, u32[]{:S(2)}, u32[]{:S(2)}) collective-permute-start(f32[1,3,1,16,128]{4,3,2,1,0:T(8,128)S(1)} %slice.1059), channel_id=1, source_target_pairs={{8,0},{16,8},{24,16},{32,24},{40,32},{48,40},{56,48},{64,56},{72,6... | collective-permute-start | bytes 73736 | tf_op jit(solution)/shard_map/ppermute | solution.py:13
  (12 other events, 81.3 us)
where the time goes:
time: 606 us; the launch traced here: 604 us
  other arithmetic  270 us (45%)
  blocking collectives  133 us (22%)
  local copies, waits for them, and re-layouts  111 us (18%)
  starting transfers between devices  47.1 us (8%)
  waiting for transfers between devices  42.1 us (7%)
    scatter-add x1, other arithmetic, on_device(): stress = fields[0, 3:].reshape(6, -1).at[:, places].add(values, mode='drop')  175 us
    all_gather x1, blocking collectives, on_device(): lax.all_gather(moments, 'sec', axis=1, tiled=True)  49.8 us
    scatter-add x4, other arithmetic, couple(): basin = newv[0].reshape(3, -1).at[:, rows_here].add(arrived)  49 us
    ppermute x20, starting transfers between devices, passed_along(): return lax.ppermute(block, axis, route)  47.1 us
    ppermute x20, waiting for transfers between devices, passed_along(): return lax.ppermute(block, axis, route)  42.1 us
    all_gather x1, blocking collectives, on_device(): lax.all_gather(moment_cells, 'sec', axis=0, tiled=True)  42 us
    all_gather x1, blocking collectives, on_device(): lax.all_gather(moment_owner, 'sec', axis=0, tiled=True)  41.3 us
    unnamed x57, local copies, waits for them, and re-layouts  36 us
  transfers between devices with their start and end apart: 20, of which 14 were waited for; matrix products, arithmetic and copies ran while one was open for 10% of the time, Pallas kernels for 0%

commit v1 on v0

--- a/solution.py
+++ b/solution.py
@@ -101,10 +101,23 @@
     segment_pos = lax.axis_index("segment")
     width_x, width_z, width_y = (fields.shape[2], fields.shape[3], fields.shape[4])
     cells_here = width_x * width_z * width_y
+
+    def time_series(u, net_axis):
+        m_next = jnp.concatenate(
+            lax.all_to_all(
+                jnp.stack([u] * lax.psum(1, axis_name=net_axis)),
+                axis_name=net_axis,
+                split_axis=0,
+                concat_axis=0,
+            ),
+            axis=0,
+        )
+        return m_next
+
     all_moments, all_owner, all_cells = (
         lax.all_gather(moments, "sec", axis=1, tiled=True),
         lax.all_gather(moment_owner, "sec", axis=0, tiled=True),
-        lax.all_gather(moment_cells, "sec", axis=0, tiled=True),
+        time_series(moment_cells, "sec"),
     )
     values = all_moments
     places = jnp.where(all_owner[:, 0] == my_section, all_cells, cells_here)

time: 606 us -> 574 us (0.947)
  blocking collectives: 133 us -> 90.5 us
  starting transfers between devices: 47.1 us -> 57.2 us
    all_gather x1 -> x0, blocking collectives: 42 us -> none  [on_device(): lax.all_gather(moment_cells, 'sec', axis=0, tiled=True)]
    all_to_all x0 -> x1, starting transfers between devices: none -> 10.1 us  [time_series(): lax.all_to_all(jnp.stack([u] * lax.psum(1, axis_name=net_axis)), axis_nam...]
  transfers between devices with their start and end apart: 20 -> 21, of which waited for: 14 -> 14; matrix products, arithmetic and copies ran while one was open for 10% -> 11% of each run, Pallas kernels for 0% -> 0%
where the time goes in v1:
time: 574 us; the launch traced here: 572 us
  other arithmetic  270 us (47%)
  local copies, waits for them, and re-layouts  111 us (19%)
  blocking collectives  90.5 us (16%)
  starting transfers between devices  57.2 us (10%)
  waiting for transfers between devices  42.1 us (7%)
    scatter-add x1, other arithmetic, on_device(): stress = fields[0, 3:].reshape(6, -1).at[:, places].add(values, mode='drop')  175 us
    all_gather x1, blocking collectives, on_device(): lax.all_gather(moments, 'sec', axis=1, tiled=True)  49.3 us
    scatter-add x4, other arithmetic, couple(): basin = newv[0].reshape(3, -1).at[:, rows_here].add(arrived)  49 us
    ppermute x20, starting transfers between devices, passed_along(): return lax.ppermute(block, axis, route)  47.1 us
    ppermute x20, waiting for transfers between devices, passed_along(): return lax.ppermute(block, axis, route)  42.1 us
    all_gather x1, blocking collectives, on_device(): lax.all_gather(moment_owner, 'sec', axis=0, tiled=True)  41.2 us
    unnamed x57, local copies, waits for them, and re-layouts  34.8 us
    gather x8, local copies, waits for them, and re-layouts, couple(): increment = (newv[0] - oldv[0]).reshape(3, -1)[:, rows_here]  30 us
  transfers between devices with their start and end apart: 21, of which 14 were waited for; matrix products, arithmetic and copies ran while one was open for 11% of the time, Pallas kernels for 0%

profile of v1, /device:TPU:124, one launch (start us, length us, event | category | flops | bytes accessed | tf_op | source)
XLA Modules:
  0.0 572.2 jit_solution(10258744910689513217)
XLA Ops:
  1.4 10.1 %all-to-all-start = ((s32[32,1,1024]{2,1,0:T(1,128)}), s32[32,1,1024]{2,1,0:T(1,128)S(1)}, u32[]{:S(2)}, u32[]{:S(2)}) async-start(s32[32,1,1024]{2,1,0:T(1,128)} %stack.180), calls=%async_computation | async-start | bytes 262144 | tf_op jit(solution)/shard_map/all_to_all | solution.py:107
  11.5 49.3 %all_gather.7 = f32[6,32768]{1,0:T(8,128)S(1)} all-gather(f32[6,1024]{1,0:T(8,128)} %param.14), channel_id=1, replica_groups=mesh['sec'=32,'depth'=4,'segment'=2] {'sec'}, dimensions={1}, use_global_device_ids=true | all-gather | bytes 811008 | tf_op jit(solution)/shard_map/all_gather | solution.py:118
  60.9 8.9 %copy.799 = f32[32768,6]{1,0:T(8,128)} copy(f32[32768,6]{0,1:T(8,128)S(1)} %multiply_bitcast_fusion) | data formatting | bytes 1572864 | tf_op jit(solution)/shard_map/mul | solution.py:124
  74.0 41.2 %all_gather.6 = s32[32768,1]{0,1:T(1,128)S(1)} all-gather(s32[1024,1]{0,1:T(1,128)S(1)} %copy-done.13), channel_id=1, replica_groups=mesh['sec'=32,'depth'=4,'segment'=2] {'sec'}, dimensions={0}, use_global_device_ids=true | all-gather | bytes 135168 | tf_op jit(solution)/shard_map/all_gather | solution.py:119
  115.4 175.0 %scatter_fusion = f32[6,4096]{0,1:T(8,128)S(1)} fusion(f32[6,4096]{0,1:T(8,128)S(1)} %bitcast.378, s32[32768]{0:T(1024)S(1)} %bitcast.434, f32[32768,6]{1,0:T(8,128)} %copy.799), kind=kCustom, calls=%fused_computation.4 | custom fusion | flops 196608 | bytes 2490368 | tf_op jit(solution)/shard_map/scatter-add | solution.py:125
  292.5 7.4 %fusion.93 = (f32[1,1,2,16,128]{1,4,3,2,0:T(8,128)}, f32[1,1,2,16,128]{1,4,3,2,0:T(8,128)}, f32[1,1,2,16,128]{1,4,3,2,0:T(8,128)}, f32[1,1,2,16,128]{1,4,3,2,0:T...) fusion(f32[1,6,2,16,128]{1,4,3,2,0:T(8,128)S(1)} %bitcast.381), kind=kLoop, calls=%fused_computation.240 | loop fusion | bytes 196608 | tf_op jit(solution)/shard_map/slice | solution.py:62
  305.6 4.6 collective-permute-start
  320.8 10.7 %fusion.3 = (f32[1,2,16,128]{3,2,1,0:T(8,128)S(1)}, f32[1,2,16,128]{3,2,1,0:T(8,128)S(1)}, pred[1,2,16,128]{3,2,1,0:T(8,128)(4,1)S(1)}, pred[1,2,16,128]{3,2,1,0...) fusion(f32[1,1,16,128]{3,2,1,0:T(8,128)S(1)} %slice.912, ...), kind=kLoop, calls=%fused_computation.29 | loop fusion | flops 233472 | bytes 229312 | tf_op jit(solution)/shard_map/add | solution.py:64
  335.4 7.0 %gather_fusion = f32[2048,3]{1,0:T(8,128)S(1)} fusion(f32[3,4096]{0,1:T(8,128)} %bitcast_subtract_fusion, s32[2048]{0:T(1024)S(1)} %get-tuple-element.103), kind=kCustom, calls=%fused_computation | custom fusion | bytes 57344 | tf_op jit(solution)/shard_map/gather | solution.py:53
  345.4 12.2 %scatter_fusion.1 = f32[3,4096]{0,1:T(8,128)S(1)} fusion(f32[3,4096]{0,1:T(8,128)S(1)} %copy.807, s32[2048]{0:T(1024)S(1)} %get-tuple-element.104, f32[2048,3]{1,0:T(8,128)S(1)} %copy.808), kind=kCustom, calls=%fused_computation.5 | custom fusion | flops 6144 | bytes 81920 | tf_op jit(solution)/shard_map/scatter-add | solution.py:55
  360.5 3.9 fusion.92
  373.7 7.1 %collective-permute-done.3 = f32[1,3,1,16,128]{4,3,2,1,0:T(8,128)S(1)} collective-permute-done((f32[1,3,1,16,128]{4,3,2,1,0:T(8,128)S(1)}, f32[1,3,1,16,128]{4,3,2,1,0:T(8,128)S(1)}, u32[]{:S(2)}, u32[]{:S(2)}) %collective-permute-start.3) | collective-permute-done | bytes 24608 | tf_op jit(solution)/shard_map/ppermute | solution.py:13
  380.8 20.8 %multiply_add_fusion.6 = (f32[1,2,16,128]{3,2,1,0:T(8,128)S(1)}, f32[1,2,16,128]{3,2,1,0:T(8,128)S(1)}, f32[1,2,16,128]{3,2,1,0:T(8,128)S(1)}, f32[1,2,16,128]{3,2,1,0:T(8,128)S(1)}) fusion(f32[1,2,16,127]{3,2,1,0:T(8,128)S(1)} %slice.939, f32[1,1,2,16,128]{4,3,2,1,0:T(8,128)S(1)} %copy.875, f32[1,1,2,16,128]{4,3,2,1,0:T(8,128)S(1)} %copy.870, ...), kind=kLoop, calls=%fused_computation.178 | loop fusion | flops 307200 | bytes 245760 | tf_op jit(solution)/shard_map/add | solution.py:87
  415.9 7.2 %gather_fusion.1 = f32[2048,3]{1,0:T(8,128)S(1)} fusion(f32[3,4096]{0,1:T(8,128)} %sub.500, s32[2048]{0:T(1024)S(1)} %get-tuple-element.103), kind=kCustom, calls=%fused_computation.1 | custom fusion | bytes 57344 | tf_op jit(solution)/shard_map/gather | solution.py:53
  426.0 12.2 %scatter_fusion.2 = f32[3,4096]{0,1:T(8,128)S(1)} fusion(f32[3,4096]{0,1:T(8,128)S(1)} %copy-done, s32[2048]{0:T(1024)S(1)} %get-tuple-element.104, f32[2048,3]{1,0:T(8,128)S(1)} %copy.821), kind=kCustom, calls=%fused_computation.6 | custom fusion | flops 6144 | bytes 81920 | tf_op jit(solution)/shard_map/scatter-add | solution.py:55
  441.1 3.9 fusion.91
  454.3 7.1 %collective-permute-done.8 = f32[1,3,1,16,128]{4,3,2,1,0:T(8,128)S(1)} collective-permute-done((f32[1,3,1,16,128]{4,3,2,1,0:T(8,128)S(1)}, f32[1,3,1,16,128]{4,3,2,1,0:T(8,128)S(1)}, u32[]{:S(2)}, u32[]{:S(2)}) %collective-permute-start.8) | collective-permute-done | bytes 24608 | tf_op jit(solution)/shard_map/ppermute | solution.py:13
  475.8 7.2 %gather_fusion.2 = f32[2048,3]{1,0:T(8,128)S(1)} fusion(f32[3,4096]{0,1:T(8,128)} %sub.519, s32[2048]{0:T(1024)S(1)} %get-tuple-element.103), kind=kCustom, calls=%fused_computation.2 | custom fusion | bytes 57344 | tf_op jit(solution)/shard_map/gather | solution.py:53
  485.9 12.2 %scatter_fusion.3 = f32[3,4096]{0,1:T(8,128)S(1)} fusion(f32[3,4096]{0,1:T(8,128)S(1)} %copy-done.1, s32[2048]{0:T(1024)S(1)} %get-tuple-element.104, f32[2048,3]{1,0:T(8,128)S(1)} %copy.834), kind=kCustom, calls=%fused_computation.7 | custom fusion | flops 6144 | bytes 81920 | tf_op jit(solution)/shard_map/scatter-add | solution.py:55
  501.0 3.9 fusion.90
  514.2 7.1 %collective-permute-done.13 = f32[1,3,1,16,128]{4,3,2,1,0:T(8,128)S(1)} collective-permute-done((f32[1,3,1,16,128]{4,3,2,1,0:T(8,128)S(1)}, f32[1,3,1,16,128]{4,3,2,1,0:T(8,128)S(1)}, u32[]{:S(2)}, u32[]{:S(2)}) %collective-permute-start.13) | collective-permute-done | bytes 24608 | tf_op jit(solution)/shard_map/ppermute | solution.py:13
  535.7 7.2 %gather_fusion.3 = f32[2048,3]{1,0:T(8,128)S(1)} fusion(f32[3,4096]{0,1:T(8,128)} %sub.538, s32[2048]{0:T(1024)S(1)} %get-tuple-element.103), kind=kCustom, calls=%fused_computation.3 | custom fusion | bytes 57344 | tf_op jit(solution)/shard_map/gather | solution.py:53
  545.7 12.2 %scatter_fusion.4 = f32[3,4096]{0,1:T(8,128)S(1)} fusion(f32[3,4096]{0,1:T(8,128)S(1)} %copy-done.2, s32[2048]{0:T(1024)S(1)} %get-tuple-element.104, f32[2048,3]{1,0:T(8,128)S(1)} %copy.847), kind=kCustom, calls=%fused_computation.8 | custom fusion | flops 6144 | bytes 81920 | tf_op jit(solution)/shard_map/scatter-add | solution.py:55
  564.2 6.6 %collective-permute-done.18 = f32[1,3,1,16,128]{4,3,2,1,0:T(8,128)S(1)} collective-permute-done((f32[1,3,1,16,128]{4,3,2,1,0:T(8,128)S(1)}, f32[1,3,1,16,128]{4,3,2,1,0:T(8,128)S(1)}, u32[]{:S(2)}, u32[]{:S(2)}) %collective-permute-start.18) | collective-permute-done | bytes 24608 | tf_op jit(solution)/shard_map/ppermute | solution.py:13
  (247 shorter events, 126.0 us)
Async XLA Ops:
  1.4 113.8 %all-to-all-start = ((s32[32,1,1024]{2,1,0:T(1,128)}), s32[32,1,1024]{2,1,0:T(1,128)S(1)}, u32[]{:S(2)}, u32[]{:S(2)}) async-start(s32[32,1,1024]{2,1,0:T(1,128)} %stack.180), calls=%async_computation | async-start | bytes 262144 | tf_op jit(solution)/shard_map/all_to_all | solution.py:107
  69.8 45.3 %copy-start.12 = (s32[2048]{0:T(1024)S(1)}, s32[2048]{0:T(1024)}, u32[]{:S(2)}) copy-start(s32[2048]{0:T(1024)} %param.17) | copy-start | bytes 24580
  300.2 20.6 %collective-permute-start.1 = (f32[1,3,2,1,128]{4,3,2,1,0:T(1,128)S(1)}, f32[1,3,2,1,128]{4,3,2,1,0:T(1,128)S(1)}, u32[]{:S(2)}, u32[]{:S(2)}) collective-permute-start(f32[1,3,2,1,128]{4,3,2,1,0:T(1,128)S(1)} %pad_maximum_fusion.8), channel_id=1, source_target_pairs={{0,2},{2,4},{4,6},{1,3},{3,5},{5,7},{8,10},{10,12},{12,14},{9,11},... | collective-permute-start | bytes 9224 | tf_op jit(solution)/shard_map/ppermute | solution.py:13
  305.6 15.1 %collective-permute-start = (f32[1,3,1,16,128]{4,3,2,1,0:T(8,128)S(1)}, f32[1,3,1,16,128]{4,3,2,1,0:T(8,128)S(1)}, u32[]{:S(2)}, u32[]{:S(2)}) collective-permute-start(f32[1,3,1,16,128]{4,3,2,1,0:T(8,128)S(1)} %pad_maximum_fusion.4), channel_id=1, source_target_pairs={{0,8},{8,16},{16,24},{24,32},{32,40},{40,48},{48,56},{56,64},{64,7... | collective-permute-start | bytes 73736 | tf_op jit(solution)/shard_map/ppermute | solution.py:13
  332.2 12.0 %copy-start.9 = (f32[16]{0:T(128)S(1)}, f32[16]{0:T(128)}, u32[]{:S(2)}) copy-start(f32[16]{0:T(128)} %param.13) | copy-start | bytes 196
  342.8 2.2 collective-permute-start.2
  357.7 15.9 %collective-permute-start.4 = (f32[1,3,2,1,128]{4,2,3,1,0:T(2,128)S(1)}, f32[1,3,2,1,128]{4,2,3,1,0:T(2,128)S(1)}, u32[]{:S(2)}, u32[]{:S(2)}) collective-permute-start(f32[1,3,2,1,128]{4,2,3,1,0:T(2,128)S(1)} %copy.877), channel_id=1, source_target_pairs={{2,0},{4,2},{6,4},{3,1},{5,3},{7,5},{10,8},{12,10},{14,12},{11,9},... | collective-permute-start | bytes 9224 | tf_op jit(solution)/shard_map/ppermute | solution.py:13
  371.7 9.0 %collective-permute-start.3 = (f32[1,3,1,16,128]{4,3,2,1,0:T(8,128)S(1)}, f32[1,3,1,16,128]{4,3,2,1,0:T(8,128)S(1)}, u32[]{:S(2)}, u32[]{:S(2)}) collective-permute-start(f32[1,3,1,16,128]{4,3,2,1,0:T(8,128)S(1)} %copy.874), channel_id=1, source_target_pairs={{8,0},{16,8},{24,16},{32,24},{40,32},{48,40},{56,48},{64,56},{72,6... | collective-permute-start | bytes 73736 | tf_op jit(solution)/shard_map/ppermute | solution.py:13
  401.6 5.5 collective-permute-start.6
  404.8 5.7 collective-permute-start.5
  415.9 10.0 %copy-start = (f32[3,4096]{0,1:T(8,128)S(1)}, f32[3,4096]{0,1:T(8,128)}, u32[]{:S(2)}) copy-start(f32[3,4096]{0,1:T(8,128)} %copy.820) | copy-start | bytes 147460
  423.5 2.1 collective-permute-start.7
  438.3 16.0 %collective-permute-start.9 = (f32[1,3,2,1,128]{4,2,3,1,0:T(2,128)S(1)}, f32[1,3,2,1,128]{4,2,3,1,0:T(2,128)S(1)}, u32[]{:S(2)}, u32[]{:S(2)}) collective-permute-start(f32[1,3,2,1,128]{4,2,3,1,0:T(2,128)S(1)} %copy.885), channel_id=1, source_target_pairs={{2,0},{4,2},{6,4},{3,1},{5,3},{7,5},{10,8},{12,10},{14,12},{11,9},... | collective-permute-start | bytes 9224 | tf_op jit(solution)/shard_map/ppermute | solution.py:13
  452.4 9.0 %collective-permute-start.8 = (f32[1,3,1,16,128]{4,3,2,1,0:T(8,128)S(1)}, f32[1,3,1,16,128]{4,3,2,1,0:T(8,128)S(1)}, u32[]{:S(2)}, u32[]{:S(2)}) collective-permute-start(f32[1,3,1,16,128]{4,3,2,1,0:T(8,128)S(1)} %copy.882), channel_id=1, source_target_pairs={{8,0},{16,8},{24,16},{32,24},{40,32},{48,40},{56,48},{64,56},{72,6... | collective-permute-start | bytes 73736 | tf_op jit(solution)/shard_map/ppermute | solution.py:13
  461.5 5.5 collective-permute-start.11
  464.7 5.7 collective-permute-start.10
  483.3 2.1 collective-permute-start.12
  498.2 16.0 %collective-permute-start.14 = (f32[1,3,2,1,128]{4,2,3,1,0:T(2,128)S(1)}, f32[1,3,2,1,128]{4,2,3,1,0:T(2,128)S(1)}, u32[]{:S(2)}, u32[]{:S(2)}) collective-permute-start(f32[1,3,2,1,128]{4,2,3,1,0:T(2,128)S(1)} %copy.893), channel_id=1, source_target_pairs={{2,0},{4,2},{6,4},{3,1},{5,3},{7,5},{10,8},{12,10},{14,12},{11,9},... | collective-permute-start | bytes 9224 | tf_op jit(solution)/shard_map/ppermute | solution.py:13
  512.2 9.0 %collective-permute-start.13 = (f32[1,3,1,16,128]{4,3,2,1,0:T(8,128)S(1)}, f32[1,3,1,16,128]{4,3,2,1,0:T(8,128)S(1)}, u32[]{:S(2)}, u32[]{:S(2)}) collective-permute-start(f32[1,3,1,16,128]{4,3,2,1,0:T(8,128)S(1)} %copy.890), channel_id=1, source_target_pairs={{8,0},{16,8},{24,16},{32,24},{40,32},{48,40},{56,48},{64,56},{72,6... | collective-permute-start | bytes 73736 | tf_op jit(solution)/shard_map/ppermute | solution.py:13
  521.4 5.5 collective-permute-start.16
  524.6 5.7 collective-permute-start.15
  543.2 2.1 collective-permute-start.17
  558.7 5.5 collective-permute-start.19
  561.8 9.0 %collective-permute-start.18 = (f32[1,3,1,16,128]{4,3,2,1,0:T(8,128)S(1)}, f32[1,3,1,16,128]{4,3,2,1,0:T(8,128)S(1)}, u32[]{:S(2)}, u32[]{:S(2)}) collective-permute-start(f32[1,3,1,16,128]{4,3,2,1,0:T(8,128)S(1)} %slice.1059), channel_id=1, source_target_pairs={{8,0},{16,8},{24,16},{32,24},{40,32},{48,40},{56,48},{64,56},{72,6... | collective-permute-start | bytes 73736 | tf_op jit(solution)/shard_map/ppermute | solution.py:13
  (13 other events, 59.5 us)
